TPU v7x, 32 devices: a whole 2x2x4 slice. The times are simulated.
32 devices in a mesh: group: 4 (over x, core), replica: 8 (over z, y).
Axes of the slice: x: 2, y: 2, z: 4, core: 2. Of those that a mesh axis runs over, the one named last changes fastest.
Arguments:
- grad_parts: bfloat16 [8, 8, 128, 512], P('replica', None, 'group'), may hold values from -1 to 1
- owner_order: int32 [8], replicated, may hold values from 0 to 7, each once
- step_count: int32 [1], replicated, may hold values from 1 to 12
- stat_old: float32 [8, 512, 512], P('replica'), as said below
- root_old: bfloat16 [8, 512, 512], P('replica'), may hold values from -0.25 to 0.25
Outputs:
- update: bfloat16 [8, 128, 512], P(None, 'group')
- stat_new: float32 [8, 512, 512], P('replica')
- root_new: bfloat16 [8, 512, 512], P('replica')
Inputs may be any that keep to these rules, and one draw needn't show every extreme that they name: `stat_old`: each matrix is symmetric positive definite.
All inputs are finite; a program needn't handle non-finite values.
Results may differ from a plain program's by a relative error of at most 0.001.
The roundings to bfloat16 on the way count: a program that leaves them out, or rounds other values in their place, can miss the bound.
Values may be sent and summed in bfloat16 or wider, within the bound.
No kernel may reach another device: no remote copies, remote signals or barrier semaphores. Data moves between devices by JAX's collectives and lax.ppermute only.
A program may use at most 64 MiB of HBM per device.

v0:
```python
import jax
import jax.numpy as jnp
from jax import lax
from jax.sharding import PartitionSpec as P

ITERS = 3
decay_rate = 0.95
epsilon = 0.001


def newton(shifted):
    identity = jnp.eye(shifted.shape[0], dtype=jnp.float32)
    frobenius = jnp.sqrt(jnp.sum(shifted * shifted))
    coupled = shifted / frobenius
    root_iter = identity * frobenius ** (-0.25)
    for repeat in range(ITERS):
        factor = (5.0 * identity - coupled) * 0.25
        root_iter = jnp.dot(root_iter, factor, precision=lax.Precision.HIGHEST)
        if repeat + 1 < ITERS:
            factor_sq = jnp.dot(factor, factor, precision=lax.Precision.HIGHEST)
            factor_quad = jnp.dot(factor_sq, factor_sq, precision=lax.Precision.HIGHEST)
            coupled = jnp.dot(factor_quad, coupled, precision=lax.Precision.HIGHEST)
    return root_iter


def local(grad_parts, owner_order, step_count, stat_old, root_old):
    local_grads = grad_parts[0]
    ordered = local_grads[owner_order]
    received = lax.all_to_all(ordered[None], "replica", split_axis=1, concat_axis=0, tiled=True)
    owned = jnp.sum(received.astype(jnp.float32), axis=0)
    partial_gram = jnp.einsum("bri,brj->bij", owned, owned, precision=lax.Precision.HIGHEST)
    products = jnp.einsum(
        "bri,bij->brj", owned.astype(jnp.bfloat16), root_old, preferred_element_type=jnp.float32
    )
    partial_norm = jnp.sum(products * products, axis=(1, 2))
    gram_matrix, update_norm = lax.psum((partial_gram, partial_norm), "group")
    grad_norm = jnp.trace(gram_matrix, axis1=1, axis2=2)
    graft_scale = jnp.sqrt(grad_norm / (update_norm + 1e-06))
    scaled = (graft_scale[:, None, None] * products).astype(jnp.bfloat16)
    gathered = lax.all_gather(scaled, "replica", axis=0, tiled=True)
    update = jnp.zeros_like(gathered).at[owner_order].set(gathered)
    stat_new = decay_rate * stat_old + (1.0 - decay_rate) * gram_matrix
    correction = 1.0 / (1.0 - decay_rate ** step_count[0].astype(jnp.float32))
    shifted = stat_new * correction + epsilon * jnp.eye(stat_new.shape[1], dtype=jnp.float32)
    root_new = lax.map(newton, shifted).astype(jnp.bfloat16)
    return (update, stat_new, root_new)


def solution(mesh):
    placed = (
        P("replica", None, "group", None),
        P(),
        P(),
        P("replica", None, None),
        P("replica", None, None),
    )
    return jax.shard_map(
        local,
        mesh=mesh,
        in_specs=placed,
        out_specs=(P(None, "group", None), P("replica", None, None), P("replica", None, None)),
        check_vma=False,
    )
```

profile of v0, /device:TPU:0, one launch (start us, length us, event | category | flops | bytes accessed | tf_op | source)
XLA Modules:
  0.0 126.4 jit_solution(15580995075982099753)
XLA Ops:
  7.2 0.0 copy-start
  7.2 0.0 all-reduce.2.cloned.1.call-start
  7.2 0.7 compare_select_fusion
  7.9 1.5 %gather_fusion = bf16[8,32,512]{2,1,0:T(8,128)(2,1)S(1)} fusion(bf16[8,32,512]{2,1,0:T(8,128)(2,1)} %bitcast.40, s32[1024]{0:T(1024)S(1)} %pad_clamp_fusion), kind=kCustom, calls=%fused_computation | custom fusion | bytes 524320 | tf_op jit(solution)/shard_map/gather | solution.py:28
  9.5 16.0 %all_to_all.4 = bf16[1,8,32,512]{3,2,0,1:T(8,128)(2,1)S(1)} all-to-all(bf16[1,8,32,512]{3,2,0,1:T(8,128)(2,1)S(1)} %bitcast.38), channel_id=1, replica_groups=mesh['group'=4,'replica'=8] {'replica'}, dimensions={1} | all-to-all | bytes 524288 | tf_op jit(solution)/shard_map/all_to_all | solution.py:29
  25.5 2.0 %convolution_bitcast_fusion = f32[1,512,512]{2,1,0:T(8,128)} fusion(f32[32,512]{1,0:T(8,128)S(1)} %convert_reduce_fusion), kind=kOutput, calls=%fused_computation.5 | convolution fusion | flops 100663296 | bytes 1114112 | tf_op jit(solution)/shard_map/bri,brj->bij/dot_general | solution.py:31
  27.5 0.0 copy-start.1
  27.5 0.0 all-reduce.2.cloned.1.call-update
  28.4 0.0 copy-done
  28.4 0.8 multiply_reduce_fusion.1
  29.2 6.3 %psum.15 = f32[1]{0:T(128)} all-reduce(f32[1]{0:T(128)} %bitcast.5), channel_id=1, replica_groups=mesh['group'=4,'replica'=8] {'group'}, use_global_device_ids=true, to_apply=%region_4.5 | all-reduce | flops 1 | bytes 8 | tf_op jit(solution)/shard_map/psum | solution.py:36
  36.1 26.8 %all-reduce.2.cloned.1.call-done = f32[1,512,512]{2,1,0:T(8,128)} async-done(((f32[1,512,512]{2,1,0:T(8,128)}), f32[1,512,512]{2,1,0:T(8,128)}) %all-reduce.2.cloned.1.call-update) | async-done | bytes 1048592 | tf_op jit(solution)/shard_map/psum | solution.py:36
  63.0 0.0 copy-done.1
  63.0 2.2 %multiply_reduce_fusion = (f32[]{:T(128)}, f32[1,512,512]{2,1,0:T(8,128)S(1)}, f32[]{:T(128)}) fusion(f32[]{:T(128)} %bitcast.8, f32[1,512,512]{2,1,0:T(8,128)} %all-reduce.2.cloned.1.call-done, f32[1,512,512]{2,1,0:T(8,128)S(1)} %copy-done.1), kind=kLoop, calls=%fused_computation.21 | loop fusion | flops 2883582 | bytes 3145740 | tf_op jit(solution)/shard_map/while/body/eval_jaxpr/reduce_sum | solution.py:13
  65.1 0.0 copy-start.2
  65.8 2.1 %fusion.6 = f32[512,512]{1,0:T(8,128)S(1)} fusion(f32[1,512,512]{2,1,0:T(8,128)S(1)} %get-tuple-element.13, f32[]{:T(128)S(6)} %sqrt.8, f32[]{:T(128)} %bitcast.8), kind=kOutput, calls=%fused_computation.12 | convolution fusion | flops 1612709888 | bytes 2097160 | tf_op jit(solution)/shard_map/while/body/eval_jaxpr/dot_general | solution.py:20
  67.9 0.0 copy-done.2
  67.9 1.8 %fusion.51 = f32[512,512]{1,0:T(8,128)S(1)} fusion(f32[512,512]{1,0:T(8,128)S(1)} %fusion.6), kind=kOutput, calls=%fused_computation.63 | convolution fusion | flops 1610612736 | bytes 2097152 | tf_op jit(solution)/shard_map/while/body/eval_jaxpr/dot_general | solution.py:21
  69.8 3.1 %fusion.8 = f32[512,512]{1,0:T(8,128)S(1)} fusion(f32[512,512]{1,0:T(8,128)S(1)} %fusion.51, f32[1,512,512]{2,1,0:T(8,128)} %copy-done.2, f32[]{:T(128)S(6)} %sqrt.8, f32[]{:T(128)} %bitcast.8), kind=kOutput, calls=%fused_computation.14 | convolution fusion | flops 1611923456 | bytes 3145736 | tf_op jit(solution)/shard_map/while/body/eval_jaxpr/dot_general | solution.py:22
  72.9 1.9 %fusion.16 = f32[512,512]{1,0:T(8,128)S(1)} fusion(f32[512,512]{1,0:T(8,128)S(1)} %fusion.8), kind=kOutput, calls=%fused_computation.28 | convolution fusion | flops 1611661312 | bytes 2097152 | tf_op jit(solution)/shard_map/while/body/eval_jaxpr/dot_general | solution.py:20
  74.9 1.8 %fusion.52 = f32[512,512]{1,0:T(8,128)S(1)} fusion(f32[512,512]{1,0:T(8,128)S(1)} %fusion.16), kind=kOutput, calls=%fused_computation.64 | convolution fusion | flops 1610612736 | bytes 2097152 | tf_op jit(solution)/shard_map/while/body/eval_jaxpr/dot_general | solution.py:21
  76.7 1.9 %fusion = f32[512,512]{1,0:T(8,128)S(1)} fusion(f32[512,512]{1,0:T(8,128)S(1)} %fusion.52, f32[512,512]{1,0:T(8,128)S(1)} %fusion.8), kind=kOutput, calls=%fused_computation.6 | convolution fusion | flops 1611661312 | bytes 3145728 | tf_op jit(solution)/shard_map/while/body/eval_jaxpr/dot_general | solution.py:22
  78.6 3.3 %fusion.3 = f32[512,512]{1,0:T(8,128)S(1)} fusion(f32[]{:T(128)S(6)} %pow.9, f32[1,512,512]{2,1,0:T(8,128)} %copy-done.2, f32[]{:T(128)S(6)} %sqrt.8, f32[]{:T(128)} %bitcast.8), kind=kOutput, calls=%fused_computation.10 | convolution fusion | flops 1613496320 | bytes 2097164 | tf_op jit(solution)/shard_map/while/body/eval_jaxpr/dot_general | solution.py:18
  82.0 1.9 %fusion.18 = f32[512,512]{1,0:T(8,128)S(1)} fusion(f32[512,512]{1,0:T(8,128)S(1)} %fusion.3, f32[512,512]{1,0:T(8,128)S(1)} %fusion.8), kind=kOutput, calls=%fused_computation.29 | convolution fusion | flops 1611661312 | bytes 3145728 | tf_op jit(solution)/shard_map/while/body/eval_jaxpr/dot_general | solution.py:18
  84.6 30.8 %all-gather = bf16[256,512]{1,0:T(8,128)(2,1)S(1)} all-gather(bf16[32,512]{1,0:T(8,128)(2,1)S(1)} %multiply_convert_fusion), channel_id=2, replica_groups=mesh['group'=4,'replica'=8] {'replica'}, dimensions={0}, use_global_device_ids=true | all-gather | bytes 294912 | tf_op jit(solution)/shard_map/all_gather | solution.py:40
  115.5 2.6 %fusion.1 = bf16[1,512,512]{2,1,0:T(8,128)(2,1)} fusion(f32[512,512]{1,0:T(8,128)S(1)} %fusion.18, f32[512,512]{1,0:T(8,128)S(1)} %fusion), kind=kOutput, calls=%fused_computation.8 | convolution fusion | flops 1610874880 | bytes 2621440 | tf_op jit(solution)/shard_map/while/body/eval_jaxpr/dot_general | solution.py:18
  118.1 0.8 scatter_fusion
  118.9 0.0 copy-start.3
  118.9 0.7 copy-done.3
  (4 shorter events, 0.1 us)
Async XLA Ops:
  7.2 21.2 %copy-start = (bf16[1,512,512]{2,1,0:T(8,128)(2,1)S(1)}, bf16[1,512,512]{2,1,0:T(8,128)(2,1)}, u32[]{:S(2)}) copy-start(bf16[1,512,512]{2,1,0:T(8,128)(2,1)} %param.9) | copy-start | bytes 1572868
  7.2 55.8 %all-reduce.2.cloned.1.call-start = ((), (), s32[]{:S(2)}) async-start(), calls=%async_computation.1 | async-start | bytes 2097152 | tf_op jit(solution)/shard_map/psum | solution.py:36
  27.5 35.4 %copy-start.1 = (f32[1,512,512]{2,1,0:T(8,128)S(1)}, f32[1,512,512]{2,1,0:T(8,128)}, u32[]{:S(2)}) copy-start(f32[1,512,512]{2,1,0:T(8,128)} %param.8) | copy-start | bytes 3145732
  65.1 2.8 %copy-start.2 = (f32[1,512,512]{2,1,0:T(8,128)}, f32[1,512,512]{2,1,0:T(8,128)S(1)}, u32[]{:S(2)}) copy-start(f32[1,512,512]{2,1,0:T(8,128)S(1)} %get-tuple-element.13) | copy-start | bytes 3145732
  118.9 0.7 copy-start.3
Sparse Core Ops, SparseCore 0:
  27.7 35.2 all-reduce.1
where the time goes:
time: 127 us; the launch traced here: 126 us
  blocking collectives  53.1 us (42%)
  waiting for transfers between devices  26.9 us (21%)
  matrix products  23.4 us (18%)
  between operations  17.1 us (13%)
  local copies, waits for them, and re-layouts  3 us (2%)
  other arithmetic  2.95 us (2%)
    all_gather x1, blocking collectives, local(): gathered = lax.all_gather(scaled, 'replica', axis=0, tiled=True)  30.8 us
    psum x1, waiting for transfers between devices, local(): gram_matrix, update_norm = lax.psum((partial_gram, partial_norm), 'group')  26.8 us
    all_to_all x1, blocking collectives, local(): lax.all_to_all(ordered[None], 'replica', split_axis=1, concat_axis=0, til...  16 us
    dot_general x3, matrix products, newton(): root_iter = jnp.dot(root_iter, factor, precision=lax.Precision.HIGHEST)  7.9 us
    psum x1, blocking collectives, local(): gram_matrix, update_norm = lax.psum((partial_gram, partial_norm), 'group')  6.27 us
    dot_general x2, matrix products, newton(): coupled = jnp.dot(factor_quad, coupled, precision=lax.Precision.HIGHEST)  5 us
    dot_general x2, matrix products, newton(): factor_sq = jnp.dot(factor, factor, precision=lax.Precision.HIGHEST)  3.98 us
    dot_general x2, matrix products, newton(): factor_quad = jnp.dot(factor_sq, factor_sq, precision=lax.Precision.HIGHEST)  3.68 us
  transfers between devices with their start and end apart: 1, of which 1 were waited for; matrix products, arithmetic and copies ran while one was open for 1% of the time, Pallas kernels for 0%

commit v1 on v0

--- a/solution.py
+++ b/solution.py
@@ -37,7 +37,9 @@
     grad_norm = jnp.trace(gram_matrix, axis1=1, axis2=2)
     graft_scale = jnp.sqrt(grad_norm / (update_norm + 1e-06))
     scaled = (graft_scale[:, None, None] * products).astype(jnp.bfloat16)
-    gathered = lax.all_gather(scaled, "replica", axis=0, tiled=True)
+    gathered = jnp.concatenate(
+        lax.all_to_all(jnp.stack([scaled] * lax.axis_size("replica")), "replica", 0, 0), axis=0
+    )
     update = jnp.zeros_like(gathered).at[owner_order].set(gathered)
     stat_new = decay_rate * stat_old + (1.0 - decay_rate) * gram_matrix
     correction = 1.0 / (1.0 - decay_rate ** step_count[0].astype(jnp.float32))

time: 127 us -> 106 us (0.83)
  blocking collectives: 53.1 us -> 22.3 us
  starting transfers between devices: 0.04 us -> 5.55 us
  waiting for transfers between devices: 26.9 us -> 29.6 us
    all_gather x1 -> x0, blocking collectives: 30.8 us -> none  [local(): gathered = lax.all_gather(scaled, 'replica', axis=0, tiled=True)]
    all_to_all x0 -> x1, starting transfers between devices: none -> 5.52 us  [local(): lax.all_to_all(jnp.stack([scaled] * lax.axis_size('replica')), 'replica',...]
    all_to_all x0 -> x1, waiting for transfers between devices: none -> 2.71 us  [local(): lax.all_to_all(jnp.stack([scaled] * lax.axis_size('replica')), 'replica',...]
    dot_general x3, matrix products: 7.9 us -> 10.1 us  [newton(): root_iter = jnp.dot(root_iter, factor, precision=lax.Precision.HIGHEST)]
  transfers between devices with their start and end apart: 1 -> 2, of which waited for: 1 -> 2; matrix products, arithmetic and copies ran while one was open for 1% -> 6% of each run, Pallas kernels for 0% -> 0%
where the time goes in v1:
time: 106 us
  waiting for transfers between devices  29.6 us (28%)
  matrix products  24.3 us (23%)
  blocking collectives  22.3 us (21%)
  between operations  17.1 us (16%)
  starting transfers between devices  5.55 us (5%)
  local copies, waits for them, and re-layouts  3.72 us (4%)
  other arithmetic  2.95 us (3%)
    psum x1, waiting for transfers between devices, local(): gram_matrix, update_norm = lax.psum((partial_gram, partial_norm), 'group')  26.8 us
    all_to_all x1, blocking collectives, local(): lax.all_to_all(ordered[None], 'replica', split_axis=1, concat_axis=0, til...  16 us
    dot_general x3, matrix products, newton(): root_iter = jnp.dot(root_iter, factor, precision=lax.Precision.HIGHEST)  10.1 us
    psum x1, blocking collectives, local(): gram_matrix, update_norm = lax.psum((partial_gram, partial_norm), 'group')  6.27 us
    all_to_all x1, starting transfers between devices, local(): lax.all_to_all(jnp.stack([scaled] * lax.axis_size('replica')), 'replica',...  5.52 us
    dot_general x2, matrix products, newton(): factor_sq = jnp.dot(factor, factor, precision=lax.Precision.HIGHEST)  3.98 us
    dot_general x2, matrix products, newton(): coupled = jnp.dot(factor_quad, coupled, precision=lax.Precision.HIGHEST)  3.77 us
    dot_general x2, matrix products, newton(): factor_quad = jnp.dot(factor_sq, factor_sq, precision=lax.Precision.HIGHEST)  3.68 us
  transfers between devices with their start and end apart: 2, of which 2 were waited for; matrix products, arithmetic and copies ran while one was open for 6% of the time, Pallas kernels for 0%

profile of v1, /device:TPU:0, one launch (start us, length us, event | category | flops | bytes accessed | tf_op | source)
XLA Modules:
  0.0 105.5 jit_solution(12619447655755354590)
XLA Ops:
  7.2 0.0 copy-start
  7.2 0.0 all-reduce.2.cloned.1.call-start
  7.2 0.7 compare_select_fusion
  7.9 1.5 %gather_fusion = bf16[8,32,512]{2,1,0:T(8,128)(2,1)S(1)} fusion(bf16[8,32,512]{2,1,0:T(8,128)(2,1)} %bitcast.40, s32[1024]{0:T(1024)S(1)} %pad_clamp_fusion), kind=kCustom, calls=%fused_computation | custom fusion | bytes 524320 | tf_op jit(solution)/shard_map/gather | solution.py:28
  9.5 16.0 %all_to_all.14 = bf16[1,8,32,512]{3,2,0,1:T(8,128)(2,1)S(1)} all-to-all(bf16[1,8,32,512]{3,2,0,1:T(8,128)(2,1)S(1)} %bitcast.38), channel_id=1, replica_groups=mesh['group'=4,'replica'=8] {'replica'}, dimensions={1} | all-to-all | bytes 524288 | tf_op jit(solution)/shard_map/all_to_all | solution.py:29
  25.5 2.0 %convolution_bitcast_fusion = f32[1,512,512]{2,1,0:T(8,128)} fusion(f32[32,512]{1,0:T(8,128)S(1)} %convert_reduce_fusion), kind=kOutput, calls=%fused_computation.5 | convolution fusion | flops 100663296 | bytes 1114112 | tf_op jit(solution)/shard_map/bri,brj->bij/dot_general | solution.py:31
  27.5 0.0 copy-start.1
  27.5 0.0 all-reduce.2.cloned.1.call-update
  28.4 0.0 copy-done
  28.4 0.8 multiply_reduce_fusion.1
  29.2 6.3 %psum.15 = f32[1]{0:T(128)} all-reduce(f32[1]{0:T(128)} %bitcast.5), channel_id=1, replica_groups=mesh['group'=4,'replica'=8] {'group'}, use_global_device_ids=true, to_apply=%region_4.5 | all-reduce | flops 1 | bytes 8 | tf_op jit(solution)/shard_map/psum | solution.py:36
  36.1 26.8 %all-reduce.2.cloned.1.call-done = f32[1,512,512]{2,1,0:T(8,128)} async-done(((f32[1,512,512]{2,1,0:T(8,128)}), f32[1,512,512]{2,1,0:T(8,128)}) %all-reduce.2.cloned.1.call-update) | async-done | bytes 1048592 | tf_op jit(solution)/shard_map/psum | solution.py:36
  63.0 0.0 copy-done.1
  63.0 2.2 %multiply_reduce_fusion = (f32[]{:T(128)}, f32[1,512,512]{2,1,0:T(8,128)S(1)}, f32[]{:T(128)}) fusion(f32[]{:T(128)} %bitcast.8, f32[1,512,512]{2,1,0:T(8,128)} %all-reduce.2.cloned.1.call-done, f32[1,512,512]{2,1,0:T(8,128)S(1)} %copy-done.1), kind=kLoop, calls=%fused_computation.21 | loop fusion | flops 2883582 | bytes 3145740 | tf_op jit(solution)/shard_map/while/body/eval_jaxpr/reduce_sum | solution.py:13
  65.1 0.0 copy-start.2
  65.8 2.1 %fusion.6 = f32[512,512]{1,0:T(8,128)S(1)} fusion(f32[1,512,512]{2,1,0:T(8,128)S(1)} %get-tuple-element.13, f32[]{:T(128)S(6)} %sqrt.8, f32[]{:T(128)} %bitcast.8), kind=kOutput, calls=%fused_computation.12 | convolution fusion | flops 1612709888 | bytes 2097160 | tf_op jit(solution)/shard_map/while/body/eval_jaxpr/dot_general | solution.py:20
  67.9 1.8 %fusion.51 = f32[512,512]{1,0:T(8,128)S(1)} fusion(f32[512,512]{1,0:T(8,128)S(1)} %fusion.6), kind=kOutput, calls=%fused_computation.63 | convolution fusion | flops 1610612736 | bytes 2097152 | tf_op jit(solution)/shard_map/while/body/eval_jaxpr/dot_general | solution.py:21
  69.8 0.0 copy-done.2
  69.8 1.9 %fusion.8 = f32[512,512]{1,0:T(8,128)S(1)} fusion(f32[512,512]{1,0:T(8,128)S(1)} %fusion.51, f32[1,512,512]{2,1,0:T(8,128)S(1)} %get-tuple-element.13, f32[]{:T(128)S(6)} %sqrt.8, f32[]{:T(128)} %bitcast.8), kind=kOutput, calls=%fused_computation.14 | convolution fusion | flops 1611923456 | bytes 3145736 | tf_op jit(solution)/shard_map/while/body/eval_jaxpr/dot_general | solution.py:22
  71.7 1.9 %fusion.16 = f32[512,512]{1,0:T(8,128)S(1)} fusion(f32[512,512]{1,0:T(8,128)S(1)} %fusion.8), kind=kOutput, calls=%fused_computation.28 | convolution fusion | flops 1611661312 | bytes 2097152 | tf_op jit(solution)/shard_map/while/body/eval_jaxpr/dot_general | solution.py:20
  73.6 1.8 %fusion.52 = f32[512,512]{1,0:T(8,128)S(1)} fusion(f32[512,512]{1,0:T(8,128)S(1)} %fusion.16), kind=kOutput, calls=%fused_computation.64 | convolution fusion | flops 1610612736 | bytes 2097152 | tf_op jit(solution)/shard_map/while/body/eval_jaxpr/dot_general | solution.py:21
  75.5 1.8 %fusion = f32[512,512]{1,0:T(8,128)S(1)} fusion(f32[512,512]{1,0:T(8,128)S(1)} %fusion.52, f32[512,512]{1,0:T(8,128)S(1)} %fusion.8), kind=kOutput, calls=%fused_computation.6 | convolution fusion | flops 1611661312 | bytes 3145728 | tf_op jit(solution)/shard_map/while/body/eval_jaxpr/dot_general | solution.py:22
  77.4 4.3 %fusion.3 = f32[512,512]{1,0:T(8,128)} fusion(f32[]{:T(128)S(6)} %pow.9, f32[1,512,512]{2,1,0:T(8,128)} %copy-done.2, f32[]{:T(128)S(6)} %sqrt.8, f32[]{:T(128)} %bitcast.8), kind=kOutput, calls=%fused_computation.10 | convolution fusion | flops 1613496320 | bytes 2097164 | tf_op jit(solution)/shard_map/while/body/eval_jaxpr/dot_general | solution.py:18
  82.5 0.7 stack.2
  83.2 5.5 %all-to-all-start.1 = ((bf16[8,1,32,512]{3,2,1,0:T(8,128)(2,1)}), bf16[8,1,32,512]{3,2,1,0:T(8,128)(2,1)S(1)}, u32[]{:S(2)}, u32[]{:S(2)}) async-start(bf16[8,1,32,512]{3,2,1,0:T(8,128)(2,1)} %stack.2), calls=%async_computation.1 | async-start | bytes 524288 | tf_op jit(solution)/shard_map/all_to_all | solution.py:41
  88.7 3.1 %fusion.18 = f32[512,512]{1,0:T(8,128)S(1)} fusion(f32[512,512]{1,0:T(8,128)} %fusion.3, f32[512,512]{1,0:T(8,128)S(1)} %fusion.8), kind=kOutput, calls=%fused_computation.29 | convolution fusion | flops 1611661312 | bytes 3145728 | tf_op jit(solution)/shard_map/while/body/eval_jaxpr/dot_general | solution.py:18
  91.9 2.6 %fusion.1 = bf16[1,512,512]{2,1,0:T(8,128)(2,1)} fusion(f32[512,512]{1,0:T(8,128)S(1)} %fusion.18, f32[512,512]{1,0:T(8,128)S(1)} %fusion), kind=kOutput, calls=%fused_computation.8 | convolution fusion | flops 1610874880 | bytes 2621440 | tf_op jit(solution)/shard_map/while/body/eval_jaxpr/dot_general | solution.py:18
  94.5 2.7 %all-to-all-done.1 = bf16[8,1,32,512]{3,2,1,0:T(8,128)(2,1)S(1)} async-done(((bf16[8,1,32,512]{3,2,1,0:T(8,128)(2,1)}), bf16[8,1,32,512]{3,2,1,0:T(8,128)(2,1)S(1)}, u32[]{:S(2)}, u32[]{:S(2)}) %all-to-all-start.1) | async-done | bytes 262176 | tf_op jit(solution)/shard_map/all_to_all | solution.py:41
  97.2 0.8 scatter_fusion
  98.0 0.0 copy-start.3
  98.0 0.7 copy-done.3
  (4 shorter events, 0.1 us)
Async XLA Ops:
  7.2 21.2 %copy-start = (bf16[1,512,512]{2,1,0:T(8,128)(2,1)S(1)}, bf16[1,512,512]{2,1,0:T(8,128)(2,1)}, u32[]{:S(2)}) copy-start(bf16[1,512,512]{2,1,0:T(8,128)(2,1)} %param.9) | copy-start | bytes 1572868
  7.2 55.8 %all-reduce.2.cloned.1.call-start = ((), (), s32[]{:S(2)}) async-start(), calls=%async_computation.2 | async-start | bytes 2097152 | tf_op jit(solution)/shard_map/psum | solution.py:36
  27.5 35.4 %copy-start.1 = (f32[1,512,512]{2,1,0:T(8,128)S(1)}, f32[1,512,512]{2,1,0:T(8,128)}, u32[]{:S(2)}) copy-start(f32[1,512,512]{2,1,0:T(8,128)} %param.8) | copy-start | bytes 3145732
  65.1 4.6 %copy-start.2 = (f32[1,512,512]{2,1,0:T(8,128)}, f32[1,512,512]{2,1,0:T(8,128)S(1)}, u32[]{:S(2)}) copy-start(f32[1,512,512]{2,1,0:T(8,128)S(1)} %get-tuple-element.13) | copy-start | bytes 3145732
  83.2 14.0 %all-to-all-start.1 = ((bf16[8,1,32,512]{3,2,1,0:T(8,128)(2,1)}), bf16[8,1,32,512]{3,2,1,0:T(8,128)(2,1)S(1)}, u32[]{:S(2)}, u32[]{:S(2)}) async-start(bf16[8,1,32,512]{3,2,1,0:T(8,128)(2,1)} %stack.2), calls=%async_computation.1 | async-start | bytes 524288 | tf_op jit(solution)/shard_map/all_to_all | solution.py:41
  98.0 0.7 copy-start.3
Sparse Core Ops, SparseCore 0:
  27.7 35.2 all-reduce.1
